TPU v7x, 256 devices: a whole 4x4x8 slice. The times are simulated.
256 devices in a mesh: gx: 64 (over z, y, x_hi), gy: 4 (over x_lo, core).
Axes of the slice: x: 4 (x_hi: 2, x_lo: 2; x = x_hi * 2 + x_lo), y: 4, z: 8, core: 2. Of those that a mesh axis runs over, the one named last changes fastest.
Arguments:
- points: bfloat16 [4, 64, 64, 32, 128], P('gy', 'gx'), may hold values from -6 to 6
- counts: int32 [4, 64, 64], P('gy', 'gx'), may hold values from 10 to 32, as said below
- voxels: int32 [4, 64, 64, 32], P('gy', 'gx'), may hold values from 0 to 1023, as said below
- occupancy: int32 [64, 4, 2], P('gx', 'gy'), may hold values from 0 to 1, as said below
- weight: bfloat16 [27, 96, 96], replicated, may hold values from -0.125 to 0.125
- w_in: bfloat16 [128, 96], replicated, may hold values from -0.5 to 0.5
- cotangent: bfloat16 [512, 32, 16, 96], P('gx', 'gy'), may hold values from -6 to 6
Outputs:
- point_feat: bfloat16 [4, 64, 64, 32, 96], P('gy', 'gx')
- point_grad: bfloat16 [4, 64, 64, 32, 128], P('gy', 'gx')
- weight_grad: float32 [27, 96, 96], replicated
Inputs may be any that keep to these rules, and one draw needn't show every extreme that they name: `counts`: in each gy row one owner receives 32 rows from every source. `voxels`: every slot's voxel lies in an occupied block of its owner tile. `occupancy`: every tile has at least one occupied block.
All inputs are finite; a program needn't handle non-finite values.
Results may differ from a plain program's by a relative error of at most 0.01.
Values may be sent and summed in bfloat16 or wider, within the bound.
A program may use at most 64 MiB of HBM per device.

v0:
```python
import jax
import jax.numpy as jnp
from jax import lax
from jax.sharding import PartitionSpec as P


def padded_2(block, sides, width):
    for axis, dim in sides:
        count = lax.axis_size(axis)
        forward = [(i, i + 1) for i in range(count - 1)]
        backward = [(target, source) for source, target in forward]
        low = lax.ppermute(
            lax.slice_in_dim(block, block.shape[dim] - width, None, axis=dim), axis, forward
        )
        high = lax.ppermute(lax.slice_in_dim(block, 0, width, axis=dim), axis, backward)
        block = jnp.concatenate([low, block, high], axis=dim)
    return block


def pad_depth(field):
    return jnp.pad(field, ((0, 0), (0, 0), (1, 1), (0, 0)))


def forward_taps(padded, weight, depth, width):
    total = jnp.zeros((64 * depth, width), jnp.float32)
    for tap in range(27):
        a, b, c = (tap // 9, tap // 3 % 3, tap % 3)
        window = padded[a : a + 8, b : b + 8, c : c + depth].reshape(-1, width)
        total = total + jnp.dot(window, weight[tap], preferred_element_type=jnp.float32)
    return total


def weight_terms(padded, grad_flat, depth, width):
    terms = []
    for tap in range(27):
        a, b, c = (tap // 9, tap // 3 % 3, tap % 3)
        window = padded[a : a + 8, b : b + 8, c : c + depth].reshape(-1, width)
        terms.append(
            lax.dot_general(
                window, grad_flat, (((0,), (0,)), ((), ())), preferred_element_type=jnp.float32
            )
        )
    return jnp.stack(terms)


def backward_taps(padded, weight, depth, width):
    total = jnp.zeros((64 * depth, width), jnp.float32)
    for tap in range(27):
        a, b, c = (tap // 9, tap // 3 % 3, tap % 3)
        window = padded[2 - a : 10 - a, 2 - b : 10 - b, 2 - c : 2 - c + depth].reshape(-1, width)
        total = total + jnp.dot(window, weight[tap].T, preferred_element_type=jnp.float32)
    return total


def on_device(points, counts, voxels, occupancy, weight, w_in, cotangent):
    width = weight.shape[2]
    feat_width = points.shape[4]
    depth = cotangent.shape[2]
    shape_slots = voxels.shape
    slots = lax.broadcasted_iota(jnp.int32, shape_slots, 3)
    got_points, got_voxels, got_counts = (
        lax.all_to_all(points, "gx", split_axis=2, concat_axis=2, tiled=True),
        lax.all_to_all(voxels, "gx", split_axis=2, concat_axis=2, tiled=True),
        lax.all_to_all(counts, "gx", split_axis=2, concat_axis=2, tiled=True),
    )
    got_valid = (slots < got_counts[..., None]).astype(jnp.float32).reshape(-1, 1)
    proj = (
        jnp.dot(got_points.reshape(-1, feat_width), w_in, preferred_element_type=jnp.float32)
        * got_valid
    ).astype(jnp.bfloat16)
    flat_index = got_voxels.reshape(-1)
    column_mask = jnp.repeat(occupancy[0, 0], 8).astype(jnp.float32)
    mask = jnp.broadcast_to(column_mask[None, None, :, None], (8, 8, depth, 1))
    summed = (
        jnp.zeros((64 * depth, width), jnp.float32).at[flat_index].add(proj.astype(jnp.float32))
    )
    feature = (summed.reshape(8, 8, depth, width) * mask).astype(jnp.bfloat16)
    grad_masked = (cotangent.astype(jnp.float32) * mask).astype(jnp.bfloat16)
    feature_pad = pad_depth(padded_2(feature, (("gx", 0), ("gy", 1)), 1))
    grad_pad = pad_depth(padded_2(grad_masked, (("gx", 0), ("gy", 1)), 1))
    mask_flat = mask.reshape(-1, 1)
    output = (forward_taps(feature_pad, weight, depth, width) * mask_flat).astype(jnp.bfloat16)
    local_grad = weight_terms(feature_pad, grad_masked.reshape(-1, width), depth, width)
    weight_grad = lax.psum(local_grad, ("gx", "gy"))
    feature_grad = (backward_taps(grad_pad, weight, depth, width) * mask_flat).astype(jnp.bfloat16)
    out_rows = (output[flat_index].astype(jnp.float32) * got_valid).astype(jnp.bfloat16)
    grad_rows = feature_grad[flat_index]
    point_rows = jnp.dot(grad_rows, w_in.T, preferred_element_type=jnp.float32) * got_valid
    sent_point = point_rows.astype(jnp.bfloat16).reshape(shape_slots + (feat_width,))
    point_feat, point_grad = (
        lax.all_to_all(
            out_rows.reshape(shape_slots + (width,)), "gx", split_axis=2, concat_axis=2, tiled=True
        ),
        lax.all_to_all(sent_point, "gx", split_axis=2, concat_axis=2, tiled=True),
    )
    return (point_feat, point_grad, weight_grad)


def solution(mesh):
    placed = (
        P("gy", "gx", None, None, None),
        P("gy", "gx", None),
        P("gy", "gx", None, None),
        P("gx", "gy", None),
        P(),
        P(),
        P("gx", "gy", None, None),
    )
    return jax.shard_map(
        on_device,
        mesh=mesh,
        in_specs=placed,
        out_specs=(P("gy", "gx", None, None, None), P("gy", "gx", None, None, None), P()),
        check_vma=False,
    )
```

profile of v0, /device:TPU:1, one launch (start us, length us, event | category | flops | bytes accessed | tf_op | source)
XLA Modules:
  0.0 468.1 jit_solution(846735209724311216)
XLA Ops:
  7.2 1.4 copy.31
  8.5 15.1 %all-to-all-start.2 = ((s32[1,1,64]{1,0,2:T(1,128)}), s32[1,1,64]{1,0,2:T(1,128)S(1)}, u32[]{:S(2)}, u32[]{:S(2)}) async-start(s32[1,1,64]{1,0,2:T(1,128)} %copy.31), calls=%async_computation.2 | async-start | bytes 65536 | tf_op jit(solution)/shard_map/all_to_all | solution.py:64
  23.7 1.4 copy.29
  25.1 9.3 %all-to-all-done.2 = s32[1,1,64]{1,0,2:T(1,128)S(1)} async-done(((s32[1,1,64]{1,0,2:T(1,128)}), s32[1,1,64]{1,0,2:T(1,128)S(1)}, u32[]{:S(2)}, u32[]{:S(2)}) %all-to-all-start.2) | async-done | bytes 288 | tf_op jit(solution)/shard_map/all_to_all | solution.py:64
  34.4 4.6 all-to-all-start
  39.0 0.7 convert_bitcast_fusion
  40.0 1.2 reduce.1
  41.4 8.4 %all-to-all-done = s32[1,1,64,32]{3,1,0,2:T(1,128)S(1)} async-done(((s32[1,1,64,32]{3,1,0,2:T(1,128)}), s32[1,1,64,32]{3,1,0,2:T(1,128)S(1)}, u32[]{:S(2)}, u32[]{:S(2)}) %all-to-all-start) | async-done | bytes 8224 | tf_op jit(solution)/shard_map/all_to_all | solution.py:63
  49.8 4.6 all-to-all-start.1
  54.5 0.5 broadcast.138
  55.0 0.7 reduce.4
  55.9 13.2 %all-to-all-done.1 = bf16[1,1,64,32,128]{4,3,1,0,2:T(8,128)(2,1)S(1)} async-done(((bf16[1,1,64,32,128]{4,3,1,0,2:T(8,128)(2,1)}), bf16[1,1,64,32,128]{4,3,1,0,2:T(8,128)(2,1)S(1)}, u32[]{:S(2)}, u32[]{:S(2)}) %all-to-all-start.1) | async-done | bytes 524320 | tf_op jit(solution)/shard_map/all_to_all | solution.py:62
  69.8 11.6 %scatter_custom_fusion = f32[1024,96]{1,0:T(8,128)S(1)} fusion(s32[2048]{0:T(1024)S(1)} %bitcast.568, f32[2048,96]{1,0:T(8,128)S(1)} %copy.32, f32[]{:T(128)} %constant.1.clone.1), kind=kCustom, calls=%fused_computation.151 | custom fusion | flops 196608 | bytes 393220 | tf_op jit(solution)/shard_map/scatter-add | solution.py:75
  81.6 1.3 collective-permute-start.1
  82.9 5.5 %collective-permute-start = (bf16[1,8,16,96]{3,2,1,0:T(8,128)(2,1)S(1)}, bf16[1,8,16,96]{3,2,1,0:T(8,128)(2,1)S(1)}, u32[]{:S(2)}, u32[]{:S(2)}) collective-permute-start(bf16[1,8,16,96]{3,2,1,0:T(8,128)(2,1)S(1)} %get-tuple-element.71), channel_id=1, source_target_pairs={{0,4},{4,8},{8,12},{12,16},{16,20},{20,24},{24,28},{28,32},{32,36}... | collective-permute-start | bytes 73736 | tf_op jit(solution)/shard_map/ppermute | solution.py:12
  88.6 1.3 collective-permute-start.5
  89.9 5.5 %collective-permute-start.4 = (bf16[1,8,16,96]{3,2,1,0:T(8,128)(2,1)S(1)}, bf16[1,8,16,96]{3,2,1,0:T(8,128)(2,1)S(1)}, u32[]{:S(2)}, u32[]{:S(2)}) collective-permute-start(bf16[1,8,16,96]{3,2,1,0:T(8,128)(2,1)S(1)} %get-tuple-element.67), channel_id=1, source_target_pairs={{0,4},{4,8},{8,12},{12,16},{16,20},{20,24},{24,28},{28,32},{32,36}... | collective-permute-start | bytes 73736 | tf_op jit(solution)/shard_map/ppermute | solution.py:12
  95.4 8.8 %collective-permute-start.3 = (bf16[10,1,16,96]{3,2,1,0:T(8,128)(2,1)S(1)}, bf16[10,1,16,96]{3,2,1,0:T(8,128)(2,1)S(1)}, u32[]{:S(2)}, u32[]{:S(2)}) collective-permute-start(bf16[10,1,16,96]{3,2,1,0:T(8,128)(2,1)S(1)} %get-tuple-element.64), channel_id=1, source_target_pairs={{1,0},{2,1},{3,2},{5,4},{6,5},{7,6},{9,8},{10,9},{11,10},{13,12},{... | collective-permute-start | bytes 92168 | tf_op jit(solution)/shard_map/ppermute | solution.py:15
  104.2 2.1 collective-permute-start.2
  106.4 0.6 pad_maximum_fusion.8
  107.0 2.2 collective-permute-start.7
  109.2 3.5 collective-permute-start.6
  113.3 1.1 fusion.190
  115.3 0.4 fusion.193
  122.1 6.2 %gather_fusion = bf16[2048,96]{1,0:T(8,128)(2,1)S(1)} fusion(bf16[1024,96]{1,0:T(8,128)(2,1)S(1)} %copy.34, s32[2048]{0:T(1024)S(1)} %broadcast_clamp_fusion), kind=kCustom, calls=%fused_computation | custom fusion | bytes 794624 | tf_op jit(solution)/shard_map/gather | solution.py:86
  128.3 1.1 fusion.39
  129.4 0.9 fusion.38
  130.3 14.4 %all-to-all-start.3 = ((bf16[1,1,64,32,96]{4,3,1,0,2:T(8,128)(2,1)}), bf16[1,1,64,32,96]{4,3,1,0,2:T(8,128)(2,1)S(1)}, u32[]{:S(2)}, u32[]{:S(2)}) async-start(bf16[1,1,64,32,96]{4,3,1,0,2:T(8,128)(2,1)} %fusion.39), calls=%async_computation.3 | async-start | bytes 1048576 | tf_op jit(solution)/shard_map/all_to_all | solution.py:91
  145.0 1.1 fusion.189
  146.8 0.9 fusion.19
  147.7 0.9 fusion.37
  148.6 0.9 fusion.36
  149.4 0.9 fusion.18
  150.3 0.9 fusion.35
  151.2 0.9 fusion.34
  152.1 0.9 fusion.17
  152.9 0.9 fusion.33
  153.8 0.9 fusion.32
  154.7 0.9 fusion.16
  155.6 0.9 fusion.31
  156.4 0.9 fusion.30
  157.3 0.9 fusion.29
  158.2 0.9 fusion.28
  159.1 0.9 fusion.27
  159.9 0.9 fusion.15
  160.8 0.9 fusion.26
  161.7 0.9 fusion.25
  162.6 0.9 fusion.14
  163.4 0.9 fusion.24
  164.4 0.4 fusion.191
  170.3 0.9 fusion.23
  171.3 6.2 %gather_fusion.1 = bf16[2048,96]{1,0:T(8,128)(2,1)S(1)} fusion(bf16[1024,96]{1,0:T(8,128)(2,1)S(1)} %copy.36, s32[2048]{0:T(1024)S(1)} %broadcast_clamp_fusion), kind=kCustom, calls=%fused_computation.1 | custom fusion | bytes 794624 | tf_op jit(solution)/shard_map/gather | solution.py:87
  177.5 0.9 fusion.13
  178.4 0.9 fusion.22
  179.3 1.2 fusion
  180.4 11.9 %all-to-all-start.4 = ((bf16[1,1,64,32,128]{4,3,1,0,2:T(8,128)(2,1)}), bf16[1,1,64,32,128]{4,3,1,0,2:T(8,128)(2,1)S(1)}, u32[]{:S(2)}, u32[]{:S(2)}) async-start(bf16[1,1,64,32,128]{4,3,1,0,2:T(8,128)(2,1)} %bitcast.89), calls=%async_computation.4 | async-start | bytes 1048576 | tf_op jit(solution)/shard_map/all_to_all | solution.py:94
  192.4 0.9 fusion.21
  193.3 0.9 fusion.12
  194.2 0.9 fusion.20
  195.1 16.9 %all-to-all-done.4 = bf16[1,1,64,32,128]{4,3,1,0,2:T(8,128)(2,1)S(1)} async-done(((bf16[1,1,64,32,128]{4,3,1,0,2:T(8,128)(2,1)}), bf16[1,1,64,32,128]{4,3,1,0,2:T(8,128)(2,1)S(1)}, u32[]{:S(2)}, u32[]{:S(2)}) %all-to-all-start.4) | async-done | bytes 524320 | tf_op jit(solution)/shard_map/all_to_all | solution.py:94
  211.9 246.7 %all-reduce.4.cloned.1.call-done = f32[27,96,96]{2,1,0:T(8,128)} async-done(((f32[27,96,96]{2,1,0:T(8,128)}), f32[27,96,96]{2,1,0:T(8,128)}) %all-reduce.4.cloned.1.call-update) | async-done | bytes 995344 | tf_op jit(solution)/shard_map/psum | solution.py:84
  458.6 0.8 copy.96
  459.4 0.8 copy.97
  460.2 1.1 copy.98
  (101 shorter events, 16.1 us)
Async XLA Ops:
  7.2 61.9 %copy-start = (bf16[128,96]{0,1:T(8,128)(2,1)S(1)}, bf16[128,96]{0,1:T(8,128)(2,1)}, u32[]{:S(2)}) copy-start(bf16[128,96]{0,1:T(8,128)(2,1)} %param.12) | copy-start | bytes 73732
  8.5 25.9 %all-to-all-start.2 = ((s32[1,1,64]{1,0,2:T(1,128)}), s32[1,1,64]{1,0,2:T(1,128)S(1)}, u32[]{:S(2)}, u32[]{:S(2)}) async-start(s32[1,1,64]{1,0,2:T(1,128)} %copy.31), calls=%async_computation.2 | async-start | bytes 65536 | tf_op jit(solution)/shard_map/all_to_all | solution.py:64
  34.4 15.4 %all-to-all-start = ((s32[1,1,64,32]{3,1,0,2:T(1,128)}), s32[1,1,64,32]{3,1,0,2:T(1,128)S(1)}, u32[]{:S(2)}, u32[]{:S(2)}) async-start(s32[1,1,64,32]{3,1,0,2:T(1,128)} %copy.29), calls=%async_computation | async-start | bytes 65536 | tf_op jit(solution)/shard_map/all_to_all | solution.py:63
  49.8 19.3 %all-to-all-start.1 = ((bf16[1,1,64,32,128]{4,3,1,0,2:T(8,128)(2,1)}), bf16[1,1,64,32,128]{4,3,1,0,2:T(8,128)(2,1)S(1)}, u32[]{:S(2)}, u32[]{:S(2)}) async-start(bf16[1,1,64,32,128]{4,3,1,0,2:T(8,128)(2,1)} %bitcast.566), calls=%async_computation.1 | async-start | bytes 1048576 | tf_op jit(solution)/shard_map/all_to_all | solution.py:62
  69.4 12.0 %copy-start.3 = (bf16[8,8,16,96]{3,2,1,0:T(8,128)(2,1)S(1)}, bf16[8,8,16,96]{3,2,1,0:T(8,128)(2,1)}, u32[]{:S(2)}) copy-start(bf16[8,8,16,96]{3,2,1,0:T(8,128)(2,1)} %param.13) | copy-start | bytes 589828
  81.6 13.8 %collective-permute-start.1 = (bf16[1,8,16,96]{3,2,1,0:T(8,128)(2,1)S(1)}, bf16[1,8,16,96]{3,2,1,0:T(8,128)(2,1)S(1)}, u32[]{:S(2)}, u32[]{:S(2)}) collective-permute-start(bf16[1,8,16,96]{3,2,1,0:T(8,128)(2,1)S(1)} %get-tuple-element.72), channel_id=1, source_target_pairs={{4,0},{8,4},{12,8},{16,12},{20,16},{24,20},{28,24},{32,28},{36,32}... | collective-permute-start | bytes 73736 | tf_op jit(solution)/shard_map/ppermute | solution.py:15
  82.9 12.5 %collective-permute-start = (bf16[1,8,16,96]{3,2,1,0:T(8,128)(2,1)S(1)}, bf16[1,8,16,96]{3,2,1,0:T(8,128)(2,1)S(1)}, u32[]{:S(2)}, u32[]{:S(2)}) collective-permute-start(bf16[1,8,16,96]{3,2,1,0:T(8,128)(2,1)S(1)} %get-tuple-element.71), channel_id=1, source_target_pairs={{0,4},{4,8},{8,12},{12,16},{16,20},{20,24},{24,28},{28,32},{32,36}... | collective-permute-start | bytes 73736 | tf_op jit(solution)/shard_map/ppermute | solution.py:12
  88.6 17.8 %collective-permute-start.5 = (bf16[1,8,16,96]{3,2,1,0:T(8,128)(2,1)S(1)}, bf16[1,8,16,96]{3,2,1,0:T(8,128)(2,1)S(1)}, u32[]{:S(2)}, u32[]{:S(2)}) collective-permute-start(bf16[1,8,16,96]{3,2,1,0:T(8,128)(2,1)S(1)} %get-tuple-element.68), channel_id=1, source_target_pairs={{4,0},{8,4},{12,8},{16,12},{20,16},{24,20},{28,24},{32,28},{36,32}... | collective-permute-start | bytes 73736 | tf_op jit(solution)/shard_map/ppermute | solution.py:15
  89.9 16.5 %collective-permute-start.4 = (bf16[1,8,16,96]{3,2,1,0:T(8,128)(2,1)S(1)}, bf16[1,8,16,96]{3,2,1,0:T(8,128)(2,1)S(1)}, u32[]{:S(2)}, u32[]{:S(2)}) collective-permute-start(bf16[1,8,16,96]{3,2,1,0:T(8,128)(2,1)S(1)} %get-tuple-element.67), channel_id=1, source_target_pairs={{0,4},{4,8},{8,12},{12,16},{16,20},{20,24},{24,28},{28,32},{32,36}... | collective-permute-start | bytes 73736 | tf_op jit(solution)/shard_map/ppermute | solution.py:12
  95.4 17.5 %collective-permute-start.3 = (bf16[10,1,16,96]{3,2,1,0:T(8,128)(2,1)S(1)}, bf16[10,1,16,96]{3,2,1,0:T(8,128)(2,1)S(1)}, u32[]{:S(2)}, u32[]{:S(2)}) collective-permute-start(bf16[10,1,16,96]{3,2,1,0:T(8,128)(2,1)S(1)} %get-tuple-element.64), channel_id=1, source_target_pairs={{1,0},{2,1},{3,2},{5,4},{6,5},{7,6},{9,8},{10,9},{11,10},{13,12},{... | collective-permute-start | bytes 92168 | tf_op jit(solution)/shard_map/ppermute | solution.py:15
  104.2 8.7 %collective-permute-start.2 = (bf16[10,1,16,96]{3,2,1,0:T(8,128)(2,1)S(1)}, bf16[10,1,16,96]{3,2,1,0:T(8,128)(2,1)S(1)}, u32[]{:S(2)}, u32[]{:S(2)}) collective-permute-start(bf16[10,1,16,96]{3,2,1,0:T(8,128)(2,1)S(1)} %get-tuple-element.63), channel_id=1, source_target_pairs={{0,1},{1,2},{2,3},{4,5},{5,6},{6,7},{8,9},{9,10},{10,11},{12,13},{... | collective-permute-start | bytes 92168 | tf_op jit(solution)/shard_map/ppermute | solution.py:12
  107.0 37.7 %collective-permute-start.7 = (bf16[10,1,16,96]{3,2,1,0:T(8,128)(2,1)}, bf16[10,1,16,96]{3,2,1,0:T(8,128)(2,1)S(1)}, u32[]{:S(2)}, u32[]{:S(2)}) collective-permute-start(bf16[10,1,16,96]{3,2,1,0:T(8,128)(2,1)} %get-tuple-element.60), channel_id=1, source_target_pairs={{1,0},{2,1},{3,2},{5,4},{6,5},{7,6},{9,8},{10,9},{11,10},{13,12},{... | collective-permute-start | bytes 92168 | tf_op jit(solution)/shard_map/ppermute | solution.py:15
  109.2 35.5 %collective-permute-start.6 = (bf16[10,1,16,96]{3,2,1,0:T(8,128)(2,1)S(1)}, bf16[10,1,16,96]{3,2,1,0:T(8,128)(2,1)S(1)}, u32[]{:S(2)}, u32[]{:S(2)}) collective-permute-start(bf16[10,1,16,96]{3,2,1,0:T(8,128)(2,1)S(1)} %get-tuple-element.59), channel_id=1, source_target_pairs={{0,1},{1,2},{2,3},{4,5},{5,6},{6,7},{8,9},{9,10},{10,11},{12,13},{... | collective-permute-start | bytes 92168 | tf_op jit(solution)/shard_map/ppermute | solution.py:12
  113.3 1.1 copy-start.1
  130.3 50.1 %all-to-all-start.3 = ((bf16[1,1,64,32,96]{4,3,1,0,2:T(8,128)(2,1)}), bf16[1,1,64,32,96]{4,3,1,0,2:T(8,128)(2,1)S(1)}, u32[]{:S(2)}, u32[]{:S(2)}) async-start(bf16[1,1,64,32,96]{4,3,1,0,2:T(8,128)(2,1)} %fusion.39), calls=%async_computation.3 | async-start | bytes 1048576 | tf_op jit(solution)/shard_map/all_to_all | solution.py:91
  180.4 31.5 %all-to-all-start.4 = ((bf16[1,1,64,32,128]{4,3,1,0,2:T(8,128)(2,1)}), bf16[1,1,64,32,128]{4,3,1,0,2:T(8,128)(2,1)S(1)}, u32[]{:S(2)}, u32[]{:S(2)}) async-start(bf16[1,1,64,32,128]{4,3,1,0,2:T(8,128)(2,1)} %bitcast.89), calls=%async_computation.4 | async-start | bytes 1048576 | tf_op jit(solution)/shard_map/all_to_all | solution.py:94
  192.4 266.3 %all-reduce.4.cloned.1.call-start = ((), (), s32[]{:S(2)}) async-start(), calls=%async_computation.5 | async-start | bytes 2654208 | tf_op jit(solution)/shard_map/psum | solution.py:84
  458.6 1.6 copy-start.2
Sparse Core Ops, SparseCore 0:
  199.2 259.4 all-reduce.3
where the time goes:
time: 469 us; the launch traced here: 468 us
  waiting for transfers between devices  295 us (63%)
  starting transfers between devices  80.9 us (17%)
  matrix products  38.1 us (8%)
  local copies, waits for them, and re-layouts  22.7 us (5%)
  other arithmetic  17.2 us (4%)
  between operations  14.6 us (3%)
    psum x1, waiting for transfers between devices, on_device(): weight_grad = lax.psum(local_grad, ('gx', 'gy'))  247 us
    dot_general x27, matrix products, weight_terms(): lax.dot_general(window, grad_flat, (((0,), (0,)), ((), ())), preferred_el...  23.6 us
    all_to_all x1, waiting for transfers between devices, on_device(): lax.all_to_all(sent_point, 'gx', split_axis=2, concat_axis=2, tiled=True)  16.9 us
    ppermute x4, starting transfers between devices, padded_2(): lax.ppermute(lax.slice_in_dim(block, block.shape[dim] - width, None, axis...  16.6 us
    all_to_all x1, starting transfers between devices, on_device(): lax.all_to_all(counts, 'gx', split_axis=2, concat_axis=2, tiled=True)  15.1 us
    all_to_all x1, starting transfers between devices, on_device(): lax.all_to_all(out_rows.reshape(shape_slots + (width,)), 'gx', split_axis...  14.4 us
    ppermute x4, starting transfers between devices, padded_2(): lax.ppermute(lax.slice_in_dim(block, 0, width, axis=dim), axis, backward)  13.6 us
    all_to_all x1, waiting for transfers between devices, on_device(): lax.all_to_all(points, 'gx', split_axis=2, concat_axis=2, tiled=True)  13.2 us
  transfers between devices with their start and end apart: 14, of which 5 were waited for; matrix products, arithmetic and copies ran while one was open for 13% of the time, Pallas kernels for 0%

commit v1 on v0

--- a/solution.py
+++ b/solution.py
@@ -81,7 +81,7 @@
     mask_flat = mask.reshape(-1, 1)
     output = (forward_taps(feature_pad, weight, depth, width) * mask_flat).astype(jnp.bfloat16)
     local_grad = weight_terms(feature_pad, grad_masked.reshape(-1, width), depth, width)
-    weight_grad = lax.psum(local_grad, ("gx", "gy"))
+    weight_grad = lax.psum(lax.psum(local_grad, axis_name="gx"), axis_name="gy")
     feature_grad = (backward_taps(grad_pad, weight, depth, width) * mask_flat).astype(jnp.bfloat16)
     out_rows = (output[flat_index].astype(jnp.float32) * got_valid).astype(jnp.bfloat16)
     grad_rows = feature_grad[flat_index]

time: 469 us -> 921 us (1.96)
  waiting for transfers between devices: 295 us -> 740 us
    psum x1 -> x2, waiting for transfers between devices: 247 us -> 709 us  [on_device(): weight_grad = lax.psum(lax.psum(local_grad, axis_name='gx'), axis_name='gy')]
    all_to_all x1, waiting for transfers between devices: 16.9 us -> 0.01 us  [on_device(): lax.all_to_all(sent_point, 'gx', split_axis=2, concat_axis=2, tiled=True)]
  transfers between devices with their start and end apart: 14 -> 15, of which waited for: 5 -> 5; matrix products, arithmetic and copies ran while one was open for 13% -> 7% of each run, Pallas kernels for 0% -> 0%
where the time goes in v1:
time: 921 us; the launch traced here: 920 us
  waiting for transfers between devices  740 us (80%)
  starting transfers between devices  81.2 us (9%)
  matrix products  38.8 us (4%)
  local copies, waits for them, and re-layouts  27.5 us (3%)
  other arithmetic  17.4 us (2%)
  between operations  14.7 us (2%)
    psum x2, waiting for transfers between devices, on_device(): weight_grad = lax.psum(lax.psum(local_grad, axis_name='gx'), axis_name='gy')  709 us
    dot_general x27, matrix products, weight_terms(): lax.dot_general(window, grad_flat, (((0,), (0,)), ((), ())), preferred_el...  23.6 us
  transfers between devices with their start and end apart: 15, of which 5 were waited for; matrix products, arithmetic and copies ran while one was open for 7% of the time, Pallas kernels for 0%

profile of v1, /device:TPU:1, one launch (start us, length us, event | category | flops | bytes accessed | tf_op | source)
XLA Modules:
  0.0 920.0 jit_solution(17451816771303071328)
XLA Ops:
  7.2 1.4 copy.31
  8.5 15.1 %all-to-all-start.2 = ((s32[1,1,64]{1,0,2:T(1,128)}), s32[1,1,64]{1,0,2:T(1,128)S(1)}, u32[]{:S(2)}, u32[]{:S(2)}) async-start(s32[1,1,64]{1,0,2:T(1,128)} %copy.31), calls=%async_computation.2 | async-start | bytes 65536 | tf_op jit(solution)/shard_map/all_to_all | solution.py:64
  23.7 1.4 copy.29
  25.1 9.3 %all-to-all-done.2 = s32[1,1,64]{1,0,2:T(1,128)S(1)} async-done(((s32[1,1,64]{1,0,2:T(1,128)}), s32[1,1,64]{1,0,2:T(1,128)S(1)}, u32[]{:S(2)}, u32[]{:S(2)}) %all-to-all-start.2) | async-done | bytes 288 | tf_op jit(solution)/shard_map/all_to_all | solution.py:64
  34.4 4.6 all-to-all-start
  39.0 0.7 convert_bitcast_fusion
  40.0 1.2 reduce.1
  41.4 8.4 all-to-all-done
  49.8 4.6 all-to-all-start.1
  54.5 0.5 broadcast.138
  55.0 0.7 reduce.4
  55.9 13.2 %all-to-all-done.1 = bf16[1,1,64,32,128]{4,3,1,0,2:T(8,128)(2,1)S(1)} async-done(((bf16[1,1,64,32,128]{4,3,1,0,2:T(8,128)(2,1)}), bf16[1,1,64,32,128]{4,3,1,0,2:T(8,128)(2,1)S(1)}, u32[]{:S(2)}, u32[]{:S(2)}) %all-to-all-start.1) | async-done | bytes 524320 | tf_op jit(solution)/shard_map/all_to_all | solution.py:62
  69.8 11.6 %scatter_custom_fusion = f32[1024,96]{1,0:T(8,128)S(1)} fusion(s32[2048]{0:T(1024)S(1)} %bitcast.568, f32[2048,96]{1,0:T(8,128)S(1)} %copy.32, f32[]{:T(128)} %constant.1.clone.1), kind=kCustom, calls=%fused_computation.151 | custom fusion | flops 196608 | bytes 393220 | tf_op jit(solution)/shard_map/scatter-add | solution.py:75
  81.6 1.3 collective-permute-start.1
  82.9 5.5 collective-permute-start
  88.6 1.3 collective-permute-start.5
  89.9 5.5 collective-permute-start.4
  95.4 8.8 collective-permute-start.3
  104.2 2.1 collective-permute-start.2
  106.4 2.2 collective-permute-start.7
  108.6 3.5 collective-permute-start.6
  112.3 0.9 pad_maximum_fusion.2
  113.4 1.1 fusion.190
  122.3 6.2 gather_fusion
  128.5 1.1 fusion.39
  129.6 0.9 fusion.38
  130.5 14.2 %all-to-all-start.3 = ((bf16[1,1,64,32,96]{4,3,1,0,2:T(8,128)(2,1)}), bf16[1,1,64,32,96]{4,3,1,0,2:T(8,128)(2,1)S(1)}, u32[]{:S(2)}, u32[]{:S(2)}) async-start(bf16[1,1,64,32,96]{4,3,1,0,2:T(8,128)(2,1)} %fusion.39), calls=%async_computation.3 | async-start | bytes 1048576 | tf_op jit(solution)/shard_map/all_to_all | solution.py:91
  145.3 2.0 fusion.189
  147.5 1.0 fusion.99
  148.7 0.9 fusion.19
  149.6 0.9 fusion.37
  150.5 0.9 fusion.36
  151.3 0.9 fusion.18
  152.2 0.9 fusion.35
  153.1 0.9 fusion.34
  153.9 0.9 fusion.17
  154.8 0.9 fusion.33
  155.7 0.9 fusion.32
  156.6 0.9 fusion.16
  157.4 0.9 fusion.31
  158.3 0.9 fusion.30
  159.2 0.9 fusion.29
  160.1 0.9 fusion.28
  160.9 0.9 fusion.27
  161.8 0.9 fusion.15
  162.7 0.9 fusion.26
  163.6 0.9 fusion.25
  164.4 0.9 fusion.14
  165.3 0.9 fusion.24
  166.2 0.9 fusion.23
  167.1 0.9 fusion.13
  167.9 0.9 fusion.22
  168.8 0.9 fusion.21
  169.7 0.9 fusion.12
  170.6 0.9 fusion.20
  172.1 0.4 copy-done.18
  181.6 6.2 gather_fusion.1
  187.8 1.2 fusion
  189.0 12.1 %all-to-all-start.4 = ((bf16[1,1,64,32,128]{4,3,1,0,2:T(8,128)(2,1)}), bf16[1,1,64,32,128]{4,3,1,0,2:T(8,128)(2,1)S(1)}, u32[]{:S(2)}, u32[]{:S(2)}) async-start(bf16[1,1,64,32,128]{4,3,1,0,2:T(8,128)(2,1)} %bitcast.89), calls=%async_computation.4 | async-start | bytes 1048576 | tf_op jit(solution)/shard_map/all_to_all | solution.py:94
  201.2 618.4 %all-reduce.5.cloned.1.call-done = f32[27,96,96]{2,1,0:T(8,128)} async-done(((f32[27,96,96]{2,1,0:T(8,128)}), f32[27,96,96]{2,1,0:T(8,128)}) %all-reduce.5.cloned.1.call-update) | async-done | bytes 995344 | tf_op jit(solution)/shard_map/psum | solution.py:84
  819.6 90.9 %all-reduce.7.cloned.1.call-done = f32[27,96,96]{2,1,0:T(8,128)} async-done(((f32[27,96,96]{2,1,0:T(8,128)}), f32[27,96,96]{2,1,0:T(8,128)}) %all-reduce.7.cloned.1.call-update) | async-done | bytes 995344 | tf_op jit(solution)/shard_map/psum | solution.py:84
  910.5 0.8 copy.97
  911.3 0.8 copy.98
  912.1 1.1 copy.99
  (140 shorter events, 20.4 us)
Async XLA Ops:
  7.2 61.9 %copy-start = (bf16[128,96]{0,1:T(8,128)(2,1)S(1)}, bf16[128,96]{0,1:T(8,128)(2,1)}, u32[]{:S(2)}) copy-start(bf16[128,96]{0,1:T(8,128)(2,1)} %param.12) | copy-start | bytes 73732
  8.5 25.9 %all-to-all-start.2 = ((s32[1,1,64]{1,0,2:T(1,128)}), s32[1,1,64]{1,0,2:T(1,128)S(1)}, u32[]{:S(2)}, u32[]{:S(2)}) async-start(s32[1,1,64]{1,0,2:T(1,128)} %copy.31), calls=%async_computation.2 | async-start | bytes 65536 | tf_op jit(solution)/shard_map/all_to_all | solution.py:64
  34.4 15.4 %all-to-all-start = ((s32[1,1,64,32]{3,1,0,2:T(1,128)}), s32[1,1,64,32]{3,1,0,2:T(1,128)S(1)}, u32[]{:S(2)}, u32[]{:S(2)}) async-start(s32[1,1,64,32]{3,1,0,2:T(1,128)} %copy.29), calls=%async_computation | async-start | bytes 65536 | tf_op jit(solution)/shard_map/all_to_all | solution.py:63
  49.8 19.3 %all-to-all-start.1 = ((bf16[1,1,64,32,128]{4,3,1,0,2:T(8,128)(2,1)}), bf16[1,1,64,32,128]{4,3,1,0,2:T(8,128)(2,1)S(1)}, u32[]{:S(2)}, u32[]{:S(2)}) async-start(bf16[1,1,64,32,128]{4,3,1,0,2:T(8,128)(2,1)} %bitcast.566), calls=%async_computation.1 | async-start | bytes 1048576 | tf_op jit(solution)/shard_map/all_to_all | solution.py:62
  69.4 12.0 %copy-start.21 = (bf16[8,8,16,96]{3,2,1,0:T(8,128)(2,1)S(1)}, bf16[8,8,16,96]{3,2,1,0:T(8,128)(2,1)}, u32[]{:S(2)}) copy-start(bf16[8,8,16,96]{3,2,1,0:T(8,128)(2,1)} %param.13) | copy-start | bytes 589828
  81.6 13.8 %collective-permute-start.1 = (bf16[1,8,16,96]{3,2,1,0:T(8,128)(2,1)S(1)}, bf16[1,8,16,96]{3,2,1,0:T(8,128)(2,1)S(1)}, u32[]{:S(2)}, u32[]{:S(2)}) collective-permute-start(bf16[1,8,16,96]{3,2,1,0:T(8,128)(2,1)S(1)} %get-tuple-element.72), channel_id=1, source_target_pairs={{4,0},{8,4},{12,8},{16,12},{20,16},{24,20},{28,24},{32,28},{36,32}... | collective-permute-start | bytes 73736 | tf_op jit(solution)/shard_map/ppermute | solution.py:15
  82.9 12.5 %collective-permute-start = (bf16[1,8,16,96]{3,2,1,0:T(8,128)(2,1)S(1)}, bf16[1,8,16,96]{3,2,1,0:T(8,128)(2,1)S(1)}, u32[]{:S(2)}, u32[]{:S(2)}) collective-permute-start(bf16[1,8,16,96]{3,2,1,0:T(8,128)(2,1)S(1)} %get-tuple-element.71), channel_id=1, source_target_pairs={{0,4},{4,8},{8,12},{12,16},{16,20},{20,24},{24,28},{28,32},{32,36}... | collective-permute-start | bytes 73736 | tf_op jit(solution)/shard_map/ppermute | solution.py:12
  88.6 17.8 %collective-permute-start.5 = (bf16[1,8,16,96]{3,2,1,0:T(8,128)(2,1)S(1)}, bf16[1,8,16,96]{3,2,1,0:T(8,128)(2,1)S(1)}, u32[]{:S(2)}, u32[]{:S(2)}) collective-permute-start(bf16[1,8,16,96]{3,2,1,0:T(8,128)(2,1)S(1)} %get-tuple-element.68), channel_id=1, source_target_pairs={{4,0},{8,4},{12,8},{16,12},{20,16},{24,20},{28,24},{32,28},{36,32}... | collective-permute-start | bytes 73736 | tf_op jit(solution)/shard_map/ppermute | solution.py:15
  89.9 16.5 %collective-permute-start.4 = (bf16[1,8,16,96]{3,2,1,0:T(8,128)(2,1)S(1)}, bf16[1,8,16,96]{3,2,1,0:T(8,128)(2,1)S(1)}, u32[]{:S(2)}, u32[]{:S(2)}) collective-permute-start(bf16[1,8,16,96]{3,2,1,0:T(8,128)(2,1)S(1)} %get-tuple-element.67), channel_id=1, source_target_pairs={{0,4},{4,8},{8,12},{12,16},{16,20},{20,24},{24,28},{28,32},{32,36}... | collective-permute-start | bytes 73736 | tf_op jit(solution)/shard_map/ppermute | solution.py:12
  95.4 17.7 %collective-permute-start.3 = (bf16[10,1,16,96]{3,2,1,0:T(8,128)(2,1)S(1)}, bf16[10,1,16,96]{3,2,1,0:T(8,128)(2,1)S(1)}, u32[]{:S(2)}, u32[]{:S(2)}) collective-permute-start(bf16[10,1,16,96]{3,2,1,0:T(8,128)(2,1)S(1)} %get-tuple-element.64), channel_id=1, source_target_pairs={{1,0},{2,1},{3,2},{5,4},{6,5},{7,6},{9,8},{10,9},{11,10},{13,12},{... | collective-permute-start | bytes 92168 | tf_op jit(solution)/shard_map/ppermute | solution.py:15
  104.2 8.9 collective-permute-start.2
  106.4 38.5 %collective-permute-start.7 = (bf16[10,1,16,96]{3,2,1,0:T(8,128)(2,1)S(1)}, bf16[10,1,16,96]{3,2,1,0:T(8,128)(2,1)S(1)}, u32[]{:S(2)}, u32[]{:S(2)}) collective-permute-start(bf16[10,1,16,96]{3,2,1,0:T(8,128)(2,1)S(1)} %get-tuple-element.60), channel_id=1, source_target_pairs={{1,0},{2,1},{3,2},{5,4},{6,5},{7,6},{9,8},{10,9},{11,10},{13,12},{... | collective-permute-start | bytes 92168 | tf_op jit(solution)/shard_map/ppermute | solution.py:15
  108.6 36.3 %collective-permute-start.6 = (bf16[10,1,16,96]{3,2,1,0:T(8,128)(2,1)S(1)}, bf16[10,1,16,96]{3,2,1,0:T(8,128)(2,1)S(1)}, u32[]{:S(2)}, u32[]{:S(2)}) collective-permute-start(bf16[10,1,16,96]{3,2,1,0:T(8,128)(2,1)S(1)} %get-tuple-element.59), channel_id=1, source_target_pairs={{0,1},{1,2},{2,3},{4,5},{5,6},{6,7},{8,9},{9,10},{10,11},{12,13},{... | collective-permute-start | bytes 92168 | tf_op jit(solution)/shard_map/ppermute | solution.py:12
  113.4 1.1 copy-start.1
  130.5 58.5 %all-to-all-start.3 = ((bf16[1,1,64,32,96]{4,3,1,0,2:T(8,128)(2,1)}), bf16[1,1,64,32,96]{4,3,1,0,2:T(8,128)(2,1)S(1)}, u32[]{:S(2)}, u32[]{:S(2)}) async-start(bf16[1,1,64,32,96]{4,3,1,0,2:T(8,128)(2,1)} %fusion.39), calls=%async_computation.3 | async-start | bytes 1048576 | tf_op jit(solution)/shard_map/all_to_all | solution.py:91
  144.7 674.9 %all-reduce.5.cloned.1.call-start = ((), (), s32[]{:S(2)}) async-start(), calls=%async_computation.5 | async-start | bytes 2654208 | tf_op jit(solution)/shard_map/psum | solution.py:84
  171.6 1.0 copy-start.18
  171.9 1.0 copy-start.17
  172.1 1.0 copy-start.2
  172.1 1.1 copy-start.20
  172.8 1.0 copy-start.16
  173.4 1.0 copy-start.15
  174.0 1.0 copy-start.14
  174.6 1.0 copy-start.13
  175.2 1.0 copy-start.12
  175.8 1.0 copy-start.11
  176.4 1.0 copy-start.10
  177.0 1.0 copy-start.9
  177.6 1.0 copy-start.8
  178.2 1.0 copy-start.7
  178.8 1.0 copy-start.6
  179.0 1.0 copy-start.19
  179.4 1.0 copy-start.5
  180.2 1.0 copy-start.4
  189.0 630.6 %all-to-all-start.4 = ((bf16[1,1,64,32,128]{4,3,1,0,2:T(8,128)(2,1)}), bf16[1,1,64,32,128]{4,3,1,0,2:T(8,128)(2,1)S(1)}, u32[]{:S(2)}, u32[]{:S(2)}) async-start(bf16[1,1,64,32,128]{4,3,1,0,2:T(8,128)(2,1)} %bitcast.89), calls=%async_computation.4 | async-start | bytes 1048576 | tf_op jit(solution)/shard_map/all_to_all | solution.py:94
  201.1 709.4 %all-reduce.7.cloned.1.call-start = ((), (), s32[]{:S(2)}) async-start(), calls=%async_computation.6 | async-start | bytes 2654208 | tf_op jit(solution)/shard_map/psum | solution.py:84
  910.5 1.6 copy-start.3
Sparse Core Ops, SparseCore 0:
  171.6 647.9 all-reduce.4
  822.3 88.2 all-reduce.6
